TPU v7x, 128 devices: a whole 4x4x4 slice. The times are simulated.
128 devices in a mesh: dp: 8 (over y, x_hi), fsdp: 16 (over z, x_lo, core).
Axes of the slice: x: 4 (x_hi: 2, x_lo: 2; x = x_hi * 2 + x_lo), y: 4, z: 4, core: 2. Of those that a mesh axis runs over, the one named last changes fastest.
Arguments:
- tokens: bfloat16 [49152, 8192], P(('dp', 'fsdp')), may hold values from -6 to 6
- frozen_value_weight: bfloat16 [8192, 1024], P('fsdp'), may hold values from -0.0625 to 0.0625
- adapter_down_weight: bfloat16 [32, 8192, 64], P('dp', 'fsdp'), may hold values from -0.0625 to 0.0625
- adapter_up_weight: bfloat16 [32, 64, 1024], P('dp', None, 'fsdp'), may hold values from -0.75 to 0.75
- output_gradient: bfloat16 [49152, 1024], P(('dp', 'fsdp')), may hold values from -6 to 6
- adapter_per_block: int32 [384], P(('dp', 'fsdp')), may hold values from 0 to 31, as said below
- block_live_count: int32 [384], P(('dp', 'fsdp')), may hold values from 1 to 128
Outputs:
- values: bfloat16 [49152, 1024], P(('dp', 'fsdp'))
- input_gradient: bfloat16 [49152, 8192], P(('dp', 'fsdp'))
- grad_down: float32 [32, 8192, 64], P('dp', 'fsdp')
- grad_up: float32 [32, 64, 1024], P('dp', None, 'fsdp')
Inputs may be any that keep to these rules, and one draw needn't show every extreme that they name: `adapter_per_block`: within the blocks of one device the adapter numbers never fall.
All inputs are finite; a program needn't handle non-finite values.
Results may differ from a plain program's by a relative error of at most 0.0038.
Values may be sent and summed in bfloat16 or wider, within the bound.
No kernel may reach another device: no remote copies, remote signals or barrier semaphores. Data moves between devices by JAX's collectives and lax.ppermute only.
A program may use at most 192 MiB of HBM per device.

v0:
```python
import jax
import jax.numpy as jnp
from jax import lax
from jax.sharding import PartitionSpec as P

adapter_scale = 0.5


def in_one_piece(arrays, axis, dim, along):
    ends, at = ([], 0)
    for a in arrays[:-1]:
        at += a.shape[along]
        ends.append(at)
    both = jnp.concatenate(arrays, axis=along)
    return tuple(jnp.split(lax.all_gather(both, axis, axis=dim, tiled=True), ends, axis=along))


def rows_first(arrays, axis, dims):
    turned = [jnp.moveaxis(a, dim, 0) for a, dim in zip(arrays, dims)]
    both = jnp.concatenate([t.reshape(len(t), -1) for t in turned], axis=1)
    result, at, outs = (lax.all_gather(both, axis, axis=0, tiled=True), 0, [])
    for t, dim in zip(turned, dims):
        piece = result[:, at : at + t[0].size].reshape(-1, *t.shape[1:])
        outs.append(jnp.moveaxis(piece, 0, dim))
        at += t[0].size
    return tuple(outs)


def cut_along(x, dim, devices):
    before, after = (x.shape[:dim], x.shape[dim + 1 :])
    return jnp.moveaxis(x.reshape(*before, devices, -1, *after), dim, 0)


def cut_rows(length, count):
    turn = length // count
    if turn >= 8:
        turn -= turn % 8
    return [turn * k for k in range(1, count)]


def in_order(parts, dim):
    parts = jnp.moveaxis(parts, 0, dim)
    dims = parts.shape
    return parts.reshape(*dims[:dim], dims[dim] * dims[dim + 1], *dims[dim + 2 :])


def several_exchanges(x, axis, pieces, split_dim, concat_dim):
    parts = cut_along(x, split_dim, lax.axis_size(axis))
    widest = max(range(1, max(2, parts.ndim - 1)), key=lambda d: parts.shape[d])
    outs = []
    for piece in jnp.split(parts, cut_rows(parts.shape[widest], pieces), axis=widest):
        if piece.size:
            outs.append(lax.all_to_all(piece, axis, split_axis=0, concat_axis=0, tiled=True))
    return in_order(jnp.concatenate(outs, axis=widest), concat_dim)


def in_one_piece_2(arrays, axis, dim, along):
    widths = [a.shape[along] for a in arrays]
    both = jnp.concatenate(arrays, axis=along)
    result = lax.psum_scatter(both, axis, scatter_dimension=dim, tiled=True)
    return tuple(jnp.split(result, [sum(widths[:k]) for k in range(1, len(widths))], axis=along))


def body(
    tokens,
    frozen_value_weight,
    adapter_down_weight,
    adapter_up_weight,
    output_gradient,
    adapter_per_block,
    block_live_count,
):
    count_dev = tokens.shape[0]
    per_dev = adapter_per_block.shape[0]
    block_rows = count_dev // per_dev
    adapter_list = adapter_down_weight.shape[0] * lax.axis_size("dp")
    piece = lax.all_gather(frozen_value_weight, "fsdp", axis=0, tiled=True)
    forward_pass = jnp.dot(tokens, piece, preferred_element_type=jnp.float32)
    portion_gradient = lax.dot_general(
        output_gradient, piece, (((1,), (1,)), ((), ())), preferred_element_type=jnp.float32
    )
    down_all, up_all = in_one_piece((adapter_down_weight, adapter_up_weight), "dp", 0, 1)
    ids_all, fill_all = rows_first((adapter_per_block, block_live_count), "fsdp", (0, 0))
    positions = jnp.arange(block_rows, dtype=jnp.int32)
    catalog = jnp.arange(adapter_list, dtype=jnp.int32)
    live_slot_mask = (positions[None, :] < fill_all[:, None]).astype(jnp.float32)[:, :, None]
    choose = (ids_all[:, None] == catalog[None, :]).astype(jnp.float32)
    down_per_block = down_all[ids_all]
    group_blocks = ids_all.shape[0]
    group_rows = group_blocks * block_rows
    x_group, dy_group = (
        lax.all_to_all(tokens, "fsdp", split_axis=1, concat_axis=0, tiled=True),
        lax.all_to_all(output_gradient, "fsdp", split_axis=1, concat_axis=0, tiled=True),
    )
    input_per_block = x_group.reshape(group_blocks, block_rows, -1)
    dy_blocks = dy_group.reshape(group_blocks, block_rows, -1)
    up_per_block = up_all[ids_all]
    down_partial = jnp.einsum(
        "gzq,gqx->gzx", input_per_block, down_per_block, preferred_element_type=jnp.float32
    )
    up_partial = jnp.einsum(
        "bkc,brc->bkr", dy_blocks, up_per_block, preferred_element_type=jnp.float32
    )
    down_total, up_total = lax.psum((down_partial, up_partial), "fsdp")
    reduced_down_output = (down_total * live_slot_mask).astype(jnp.bfloat16)
    reduced_output_gradient = (up_total * live_slot_mask).astype(jnp.bfloat16)
    raised_rows = (
        jnp.einsum(
            "bkr,brc->bkc", reduced_down_output, up_per_block, preferred_element_type=jnp.float32
        )
        .astype(jnp.bfloat16)
        .reshape(group_rows, -1)
    )
    spread_input = (
        jnp.einsum(
            "qjz,qaz->qja",
            reduced_output_gradient,
            down_per_block,
            preferred_element_type=jnp.float32,
        )
        .astype(jnp.bfloat16)
        .reshape(group_rows, -1)
    )
    raised_resident, input_resident = (
        several_exchanges(raised_rows, "fsdp", 2, 0, 1),
        several_exchanges(spread_input, "fsdp", 2, 0, 1),
    )
    up_terms = jnp.einsum(
        "bkr,bkc->brc", reduced_down_output, dy_blocks, preferred_element_type=jnp.float32
    )
    up_gradient = jnp.einsum("ba,brc->arc", choose, up_terms, precision=lax.Precision.HIGHEST)
    down_gradient_terms = jnp.einsum(
        "uia,uiw->uaw", input_per_block, reduced_output_gradient, preferred_element_type=jnp.float32
    )
    down_gradient = jnp.einsum(
        "ba,bdr->adr", choose, down_gradient_terms, precision=lax.Precision.HIGHEST
    )
    grad_down, grad_up = in_one_piece_2(
        (adapter_scale * down_gradient, adapter_scale * up_gradient), "dp", 0, 1
    )
    values = (forward_pass + adapter_scale * raised_resident.astype(jnp.float32)).astype(
        jnp.bfloat16
    )
    input_gradient = (portion_gradient + adapter_scale * input_resident.astype(jnp.float32)).astype(
        jnp.bfloat16
    )
    return (values, input_gradient, grad_down, grad_up)


def solution(mesh):
    placed = (
        P(("dp", "fsdp"), None),
        P("fsdp", None),
        P("dp", "fsdp", None),
        P("dp", None, "fsdp"),
        P(("dp", "fsdp"), None),
        P(("dp", "fsdp")),
        P(("dp", "fsdp")),
    )
    return jax.shard_map(
        body,
        mesh=mesh,
        in_specs=placed,
        out_specs=(
            P(("dp", "fsdp"), None),
            P(("dp", "fsdp"), None),
            P("dp", "fsdp", None),
            P("dp", None, "fsdp"),
        ),
        check_vma=False,
    )
```

profile of v0, /device:TPU:1, one launch (start us, length us, event | category | flops | bytes accessed | tf_op | source)
XLA Modules:
  0.0 559.3 jit_solution(6873364627100419224)
XLA Ops:
  9.5 7.8 %all-to-all-start.3 = ((bf16[384,16,64]{0,2,1:T(8,128)(2,1)}), bf16[384,16,64]{0,2,1:T(8,128)(2,1)S(1)}, u32[]{:S(2)}, u32[]{:S(2)}) async-start(bf16[384,16,64]{0,2,1:T(8,128)(2,1)} %bitcast.10), calls=%async_computation.3 | async-start | bytes 1572864 | tf_op jit(solution)/shard_map/all_to_all | solution.py:93
  17.2 6.2 %copy.68 = bf16[48,16,8,512]{3,2,0,1:T(8,128)(2,1)} copy(bf16[48,16,8,512]{3,2,1,0:T(8,128)(2,1)} %bitcast.57) | data formatting | bytes 12582912 | tf_op jit(solution)/shard_map/all_to_all | solution.py:92
  23.4 6.8 %all-to-all-done.3 = bf16[384,16,64]{0,2,1:T(8,128)(2,1)S(1)} async-done(((bf16[384,16,64]{0,2,1:T(8,128)(2,1)}), bf16[384,16,64]{0,2,1:T(8,128)(2,1)S(1)}, u32[]{:S(2)}, u32[]{:S(2)}) %all-to-all-start.3) | async-done | bytes 786464 | tf_op jit(solution)/shard_map/all_to_all | solution.py:93
  30.2 5.4 all-to-all-start
  36.6 99.6 %all-gather = s32[16,3,2]{1,2,0:T(2,128)S(1)} all-gather(s32[1,3,2]{1,2,0:T(2,128)S(1)} %add_bitcast_fusion), channel_id=1, replica_groups=mesh['dp'=8,'fsdp'=16] {'fsdp'}, dimensions={0}, use_global_device_ids=true | all-gather | bytes 408 | tf_op jit(solution)/shard_map/all_gather | solution.py:21
  147.7 6.2 %convolution_bitcast_fusion.2 = f32[48,128,64]{1,2,0:T(8,128)} fusion(bf16[48,512,64]{1,2,0:T(8,128)(2,1)S(1)} %gather_fusion, bf16[48,128,512]{2,1,0:T(8,128)(2,1)} %bitcast.5), kind=kOutput, calls=%fused_computation.16 | convolution fusion | flops 402653184 | bytes 11010048 | tf_op jit(solution)/shard_map/gzq,gqx->gzx/dot_general | solution.py:98
  154.2 127.4 %all-reduce.3.cloned.1.call-done = (f32[48,128,64]{1,2,0:T(8,128)}, f32[48,128,64]{1,2,0:T(8,128)}) async-done(((f32[48,128,64]{1,2,0:T(8,128)}, f32[48,128,64]{1,2,0:T(8,128)}), (f32[48,128,64]{1,2,0:T(8,128)}, f32[48,128,64]{1,2,0:T(8,128)})) %all-reduce.3.cloned.1.call-update) | async-done | bytes 3145744 | tf_op jit(solution)/shard_map/psum | solution.py:104
  288.1 4.4 convolution_bitcast_fusion
  293.2 6.7 %fusion.2 = f32[32,512,64]{1,0,2:T(8,128)S(1)} fusion(f32[48,512,64]{1,2,0:T(8,128)S(1)} %convolution_bitcast_fusion, s32[48]{0:T(128)S(1)} %get-tuple-element.22), kind=kOutput, calls=%fused_computation.10 | convolution fusion | flops 605029888 | bytes 10485952 | tf_op jit(solution)/shard_map/ba,bdr->adr/dot_general | solution.py:135
  300.5 5.6 %copy.51 = f32[32,576,64]{1,2,0:T(8,128)} copy(f32[32,576,64]{1,0,2:T(8,128)S(1)} %pad_maximum_fusion) | data formatting | bytes 9437184 | tf_op jit(solution)/shard_map/concatenate | solution.py:59
  315.5 6.2 %all-to-all-start.1 = ((bf16[16,192,64]{1,2,0:T(8,128)(2,1)}), bf16[16,192,64]{1,2,0:T(8,128)(2,1)}, u32[]{:S(2)}, u32[]{:S(2)}) async-start(bf16[16,192,64]{1,2,0:T(8,128)(2,1)} %copy.39), calls=%async_computation.1 | async-start | bytes 1048576 | tf_op jit(solution)/shard_map/all_to_all | solution.py:53
  323.7 6.0 %convolution_convert_fusion = bf16[48,128,512]{2,1,0:T(8,128)(2,1)} fusion(bf16[48,512,64]{1,2,0:T(8,128)(2,1)S(1)} %gather_fusion, f32[48,128,64]{1,2,0:T(8,128)} %get-tuple-element.17, f32[48,128]{1,0:T(8,128)S(1)} %fusion.8), kind=kOutput, calls=%fused_computation.8 | convolution fusion | flops 406585344 | bytes 11034624 | tf_op jit(solution)/shard_map/qjz,qaz->qja/dot_general | solution.py:115
  329.7 3.9 all-to-all-done.1
  333.6 3.9 all-to-all-start.2
  337.5 6.3 %fusion.15 = (bf16[16,192,512]{2,1,0:T(8,128)(2,1)}, bf16[16,192,512]{2,1,0:T(8,128)(2,1)}) fusion(bf16[16,384,512]{2,1,0:T(8,128)(2,1)} %bitcast.55), kind=kLoop, calls=%fused_computation.35 | loop fusion | bytes 12582912 | tf_op jit(solution)/shard_map/split | solution.py:51
  343.8 7.0 %all-to-all-done.2 = bf16[16,192,64]{1,2,0:T(8,128)(2,1)S(1)} async-done(((bf16[16,192,64]{1,2,0:T(8,128)(2,1)}), bf16[16,192,64]{1,2,0:T(8,128)(2,1)S(1)}, u32[]{:S(2)}, u32[]{:S(2)}) %all-to-all-start.2) | async-done | bytes 393248 | tf_op jit(solution)/shard_map/all_to_all | solution.py:53
  351.6 49.6 %all_to_all.52 = bf16[16,192,512]{2,1,0:T(8,128)(2,1)S(1)} all-to-all(bf16[16,192,512]{2,1,0:T(8,128)(2,1)} %get-tuple-element.18), channel_id=1, replica_groups=mesh['dp'=8,'fsdp'=16] {'fsdp'}, dimensions={0} | all-to-all | bytes 6291456 | tf_op jit(solution)/shard_map/all_to_all | solution.py:53
  401.2 4.8 all-to-all-start.5
  411.7 42.0 %all-to-all-done.5 = bf16[16,192,512]{2,1,0:T(8,128)(2,1)} async-done(((bf16[16,192,512]{2,1,0:T(8,128)(2,1)}), bf16[16,192,512]{2,1,0:T(8,128)(2,1)}, u32[]{:S(2)}, u32[]{:S(2)}) %all-to-all-start.5) | async-done | bytes 3145760 | tf_op jit(solution)/shard_map/all_to_all | solution.py:53
  453.7 8.2 %multiply_bitcast_fusion = f32[16,48,8,512]{3,2,1,0:T(8,128)} fusion(bf16[16,192,512]{2,1,0:T(8,128)(2,1)} %all-to-all-done.5, bf16[16,192,512]{2,1,0:T(8,128)(2,1)S(1)} %all_to_all.52), kind=kLoop, calls=%fused_computation.3 | loop fusion | flops 15728640 | bytes 18874368
  461.9 11.8 %copy.58 = f32[16,48,8,512]{3,2,0,1:T(8,128)} copy(f32[16,48,8,512]{3,2,1,0:T(8,128)} %multiply_bitcast_fusion) | data formatting | bytes 25165824 | tf_op jit(solution)/shard_map/mul | solution.py:144
  477.2 48.3 %all-gather.4.cloned.1.call-done = bf16[8192,1024]{1,0:T(8,128)(2,1)} async-done(((bf16[512,1024]{1,0:T(8,128)(2,1)}), bf16[8192,1024]{1,0:T(8,128)(2,1)}) %all-gather.4.cloned.1.call-update) | async-done | bytes 16777232 | tf_op jit(solution)/shard_map/all_gather | solution.py:77
  525.5 12.8 %add_convert_fusion.1 = bf16[384,1024]{1,0:T(8,128)(2,1)} fusion(f32[384,1024]{1,0:T(8,128)S(1)} %copy-done.3, bf16[384,8192]{1,0:T(8,128)(2,1)} %param.7, bf16[8192,1024]{1,0:T(8,128)(2,1)} %all-gather.4.cloned.1.call-done), kind=kOutput, calls=%fused_computation.12 | convolution fusion | flops 6443237376 | bytes 25427968 | tf_op jit(solution)/shard_map/dot_general | solution.py:78
  538.3 14.5 %add_convert_fusion = bf16[384,8192]{1,0:T(8,128)(2,1)} fusion(f32[384,8192]{1,0:T(8,128)} %bitcast.56, bf16[384,1024]{1,0:T(8,128)(2,1)S(1)} %copy-done.4, bf16[8192,1024]{1,0:T(8,128)(2,1)} %all-gather.4.cloned.1.call-done), kind=kOutput, calls=%fused_computation.2 | convolution fusion | flops 6448742400 | bytes 36438016 | tf_op jit(solution)/shard_map/dot_general | solution.py:79
  (60 shorter events, 44.2 us)
Async XLA Ops:
  9.5 20.7 %all-to-all-start.3 = ((bf16[384,16,64]{0,2,1:T(8,128)(2,1)}), bf16[384,16,64]{0,2,1:T(8,128)(2,1)S(1)}, u32[]{:S(2)}, u32[]{:S(2)}) async-start(bf16[384,16,64]{0,2,1:T(8,128)(2,1)} %bitcast.10), calls=%async_computation.3 | async-start | bytes 1572864 | tf_op jit(solution)/shard_map/all_to_all | solution.py:93
  30.2 5.5 copy-start.6
  30.2 5.6 copy-start.5
  30.2 6.4 %copy-start.7 = (s32[3]{0:T(128)S(1)}, s32[3]{0:T(128)}, u32[]{:S(2)}) copy-start(s32[3]{0:T(128)} %param.13) | copy-start | bytes 40
  30.2 6.4 %copy-start.8 = (s32[3]{0:T(128)S(1)}, s32[3]{0:T(128)}, u32[]{:S(2)}) copy-start(s32[3]{0:T(128)} %param.12) | copy-start | bytes 40
  30.2 117.5 %all-to-all-start = ((bf16[384,16,512]{2,0,1:T(8,128)(2,1)}), bf16[384,16,512]{2,0,1:T(8,128)(2,1)}, u32[]{:S(2)}, u32[]{:S(2)}) async-start(bf16[384,16,512]{2,0,1:T(8,128)(2,1)} %bitcast.54), calls=%async_computation | async-start | bytes 12582912 | tf_op jit(solution)/shard_map/all_to_all | solution.py:92
  35.6 102.5 %all-gather.6.cloned.1.call-start = ((), (), s32[]{:S(2)}) async-start(), calls=%async_computation.8 | async-start | bytes 2949120 | tf_op jit(solution)/shard_map/all_gather | solution.py:15
  36.6 245.1 %all-reduce.3.cloned.1.call-start = ((), (), s32[]{:S(2)}) async-start(), calls=%async_computation.10 | async-start | bytes 6291456 | tf_op jit(solution)/shard_map/psum | solution.py:104
  138.1 2.8 copy-start.1
  153.9 319.7 %reduce-scatter.2.cloned.1.call-start = ((), (), s32[]{:S(2)}) async-start(), calls=%async_computation.9 | async-start | bytes 5898240 | tf_op jit(solution)/shard_map/reduce_scatter | solution.py:60
  288.1 4.4 copy-start
  306.1 219.3 %all-gather.4.cloned.1.call-start = ((), (), s32[]{:S(2)}) async-start(), calls=%async_computation.7 | async-start | bytes 17825792 | tf_op jit(solution)/shard_map/all_gather | solution.py:77
  315.5 18.1 %all-to-all-start.1 = ((bf16[16,192,64]{1,2,0:T(8,128)(2,1)}), bf16[16,192,64]{1,2,0:T(8,128)(2,1)}, u32[]{:S(2)}, u32[]{:S(2)}) async-start(bf16[16,192,64]{1,2,0:T(8,128)(2,1)} %copy.39), calls=%async_computation.1 | async-start | bytes 1048576 | tf_op jit(solution)/shard_map/all_to_all | solution.py:53
  333.6 17.2 %all-to-all-start.2 = ((bf16[16,192,64]{1,2,0:T(8,128)(2,1)}), bf16[16,192,64]{1,2,0:T(8,128)(2,1)S(1)}, u32[]{:S(2)}, u32[]{:S(2)}) async-start(bf16[16,192,64]{1,2,0:T(8,128)(2,1)} %copy.40), calls=%async_computation.2 | async-start | bytes 1048576 | tf_op jit(solution)/shard_map/all_to_all | solution.py:53
  350.8 0.8 copy-start.2
  401.2 52.5 %all-to-all-start.5 = ((bf16[16,192,512]{2,1,0:T(8,128)(2,1)}), bf16[16,192,512]{2,1,0:T(8,128)(2,1)}, u32[]{:S(2)}, u32[]{:S(2)}) async-start(bf16[16,192,512]{2,1,0:T(8,128)(2,1)} %get-tuple-element.19), calls=%async_computation.5 | async-start | bytes 6291456 | tf_op jit(solution)/shard_map/all_to_all | solution.py:53
  461.9 63.6 %copy-start.3 = (f32[384,1024]{1,0:T(8,128)S(1)}, f32[384,1024]{1,0:T(8,128)}, u32[]{:S(2)}) copy-start(f32[384,1024]{1,0:T(8,128)} %copy.41) | copy-start | bytes 4718596
  477.2 61.1 %copy-start.4 = (bf16[384,1024]{1,0:T(8,128)(2,1)S(1)}, bf16[384,1024]{1,0:T(8,128)(2,1)}, u32[]{:S(2)}) copy-start(bf16[384,1024]{1,0:T(8,128)(2,1)} %param.11) | copy-start | bytes 2359300
Sparse Core Ops, SparseCore 0:
  39.3 76.9 all-gather.5
  154.1 127.5 all-reduce.2
  306.2 116.6 reduce-scatter.1
  424.5 100.9 all-gather.3
where the time goes:
time: 560 us; the launch traced here: 559 us
  waiting for transfers between devices  236 us (42%)
  blocking collectives  149 us (27%)
  local copies, waits for them, and re-layouts  60.1 us (11%)
  matrix products  59.4 us (11%)
  starting transfers between devices  28.5 us (5%)
  between operations  13.9 us (2%)
  other arithmetic  12.3 us (2%)
    psum x1, waiting for transfers between devices, body(): down_total, up_total = lax.psum((down_partial, up_partial), 'fsdp')  127 us
    all_gather x1, blocking collectives, rows_first(): result, at, outs = (lax.all_gather(both, axis, axis=0, tiled=True), 0, [])  99.6 us
    all_to_all x3, waiting for transfers between devices, several_exchanges(): lax.all_to_all(piece, axis, split_axis=0, concat_axis=0, tiled=True)  52.9 us
    all_to_all x1, blocking collectives, several_exchanges(): lax.all_to_all(piece, axis, split_axis=0, concat_axis=0, tiled=True)  49.6 us
    all_gather x1, waiting for transfers between devices, body(): piece = lax.all_gather(frozen_value_weight, 'fsdp', axis=0, tiled=True)  48.3 us
    all_to_all x3, starting transfers between devices, several_exchanges(): lax.all_to_all(piece, axis, split_axis=0, concat_axis=0, tiled=True)  15 us
    dot_general x1, matrix products, body(): lax.dot_general(output_gradient, piece, (((1,), (1,)), ((), ())), preferr...  14.5 us
    dot_general x1, matrix products, body(): forward_pass = jnp.dot(tokens, piece, preferred_element_type=jnp.float32)  12.8 us
  transfers between devices with their start and end apart: 9, of which 6 were waited for; matrix products, arithmetic and copies ran while one was open for 13% of the time, Pallas kernels for 0%

commit v1 on v0

--- a/solution.py
+++ b/solution.py
@@ -74,7 +74,10 @@
     per_dev = adapter_per_block.shape[0]
     block_rows = count_dev // per_dev
     adapter_list = adapter_down_weight.shape[0] * lax.axis_size("dp")
-    piece = lax.all_gather(frozen_value_weight, "fsdp", axis=0, tiled=True)
+    piece = jnp.concatenate(
+        lax.all_to_all(jnp.stack([frozen_value_weight] * lax.axis_size("fsdp")), "fsdp", 0, 0),
+        axis=0,
+    )
     forward_pass = jnp.dot(tokens, piece, preferred_element_type=jnp.float32)
     portion_gradient = lax.dot_general(
         output_gradient, piece, (((1,), (1,)), ((), ())), preferred_element_type=jnp.float32

time: 560 us -> 677 us (1.21)
  waiting for transfers between devices: 236 us -> 309 us
  blocking collectives: 149 us -> 185 us
    all_to_all x0 -> x1, waiting for transfers between devices: none -> 169 us  [body(): lax.all_to_all(jnp.stack([frozen_value_weight] * lax.axis_size('fsdp')),...]
    all_gather x1 -> x0, waiting for transfers between devices: 48.3 us -> none  [body(): piece = lax.all_gather(frozen_value_weight, 'fsdp', axis=0, tiled=True)]
    all_to_all x3 -> x2, waiting for transfers between devices: 52.9 us -> 5.78 us  [several_exchanges(): lax.all_to_all(piece, axis, split_axis=0, concat_axis=0, tiled=True)]
    all_to_all x1 -> x2, blocking collectives: 49.6 us -> 85.3 us  [several_exchanges(): lax.all_to_all(piece, axis, split_axis=0, concat_axis=0, tiled=True)]
    all_to_all x3 -> x2, starting transfers between devices: 15 us -> 10.8 us  [several_exchanges(): lax.all_to_all(piece, axis, split_axis=0, concat_axis=0, tiled=True)]
  transfers between devices with their start and end apart: 9 -> 8, of which waited for: 6 -> 5; matrix products, arithmetic and copies ran while one was open for 13% -> 16% of each run, Pallas kernels for 0% -> 0%
where the time goes in v1:
time: 677 us; the launch traced here: 676 us
  waiting for transfers between devices  309 us (46%)
  blocking collectives  185 us (27%)
  local copies, waits for them, and re-layouts  65.5 us (10%)
  matrix products  60.4 us (9%)
  starting transfers between devices  30.2 us (4%)
  between operations  13.9 us (2%)
  other arithmetic  12.3 us (2%)
    all_to_all x1, waiting for transfers between devices, body(): lax.all_to_all(jnp.stack([frozen_value_weight] * lax.axis_size('fsdp')),...  169 us
    psum x1, waiting for transfers between devices, body(): down_total, up_total = lax.psum((down_partial, up_partial), 'fsdp')  127 us
    all_gather x1, blocking collectives, rows_first(): result, at, outs = (lax.all_gather(both, axis, axis=0, tiled=True), 0, [])  99.6 us
    all_to_all x2, blocking collectives, several_exchanges(): lax.all_to_all(piece, axis, split_axis=0, concat_axis=0, tiled=True)  85.3 us
    dot_general x1, matrix products, body(): lax.dot_general(output_gradient, piece, (((1,), (1,)), ((), ())), preferr...  14.6 us
  transfers between devices with their start and end apart: 8, of which 5 were waited for; matrix products, arithmetic and copies ran while one was open for 16% of the time, Pallas kernels for 0%

profile of v1, /device:TPU:1, one launch (start us, length us, event | category | flops | bytes accessed | tf_op | source)
XLA Modules:
  0.0 675.9 jit_solution(9823186002811572232)
XLA Ops:
  9.5 7.8 %all-to-all-start.4 = ((bf16[384,16,64]{0,2,1:T(8,128)(2,1)}), bf16[384,16,64]{0,2,1:T(8,128)(2,1)S(1)}, u32[]{:S(2)}, u32[]{:S(2)}) async-start(bf16[384,16,64]{0,2,1:T(8,128)(2,1)} %bitcast.11), calls=%async_computation.4 | async-start | bytes 1572864 | tf_op jit(solution)/shard_map/all_to_all | solution.py:96
  17.2 6.2 copy.68
  23.4 6.8 %all-to-all-done.4 = bf16[384,16,64]{0,2,1:T(8,128)(2,1)S(1)} async-done(((bf16[384,16,64]{0,2,1:T(8,128)(2,1)}), bf16[384,16,64]{0,2,1:T(8,128)(2,1)S(1)}, u32[]{:S(2)}, u32[]{:S(2)}) %all-to-all-start.4) | async-done | bytes 786464 | tf_op jit(solution)/shard_map/all_to_all | solution.py:96
  30.2 5.4 all-to-all-start.1
  36.6 99.6 %all-gather = s32[16,3,2]{1,2,0:T(2,128)S(1)} all-gather(s32[1,3,2]{1,2,0:T(2,128)S(1)} %add_bitcast_fusion), channel_id=1, replica_groups=mesh['dp'=8,'fsdp'=16] {'fsdp'}, dimensions={0}, use_global_device_ids=true | all-gather | bytes 408 | tf_op jit(solution)/shard_map/all_gather | solution.py:21
  147.7 6.2 convolution_bitcast_fusion.2
  154.0 127.1 %all-reduce.3.cloned.1.call-done = (f32[48,128,64]{1,2,0:T(8,128)}, f32[48,128,64]{1,2,0:T(8,128)}) async-done(((f32[48,128,64]{1,2,0:T(8,128)}, f32[48,128,64]{1,2,0:T(8,128)}), (f32[48,128,64]{1,2,0:T(8,128)}, f32[48,128,64]{1,2,0:T(8,128)})) %all-reduce.3.cloned.1.call-update) | async-done | bytes 3145744 | tf_op jit(solution)/shard_map/psum | solution.py:107
  289.9 6.2 all-to-all-start.2
  298.1 5.9 convolution_convert_fusion
  306.1 4.5 all-to-all-start.3
  310.6 6.1 fusion.15
  316.8 3.7 all-to-all-done.3
  321.3 42.9 %all_to_all.57 = bf16[16,192,512]{2,1,0:T(8,128)(2,1)S(1)} all-to-all(bf16[16,192,512]{2,1,0:T(8,128)(2,1)} %get-tuple-element.18), channel_id=1, replica_groups=mesh['dp'=8,'fsdp'=16] {'fsdp'}, dimensions={0} | all-to-all | bytes 6291456 | tf_op jit(solution)/shard_map/all_to_all | solution.py:53
  364.2 42.4 %all_to_all.58 = bf16[16,192,512]{2,1,0:T(8,128)(2,1)} all-to-all(bf16[16,192,512]{2,1,0:T(8,128)(2,1)S(1)} %copy-done), channel_id=1, replica_groups=mesh['dp'=8,'fsdp'=16] {'fsdp'}, dimensions={0} | all-to-all | bytes 6291456 | tf_op jit(solution)/shard_map/all_to_all | solution.py:53
  406.7 6.0 stack.2
  412.6 6.0 all-to-all-start
  427.6 3.8 convolution_bitcast_fusion
  431.4 6.7 fusion.2
  438.7 5.7 copy.51
  450.0 8.2 %multiply_bitcast_fusion = f32[16,48,8,512]{3,2,1,0:T(8,128)} fusion(bf16[16,192,512]{2,1,0:T(8,128)(2,1)} %all_to_all.58, bf16[16,192,512]{2,1,0:T(8,128)(2,1)S(1)} %all_to_all.57), kind=kLoop, calls=%fused_computation.3 | loop fusion | flops 15728640 | bytes 18874368
  458.2 11.4 %copy.58 = f32[16,48,8,512]{3,2,0,1:T(8,128)} copy(f32[16,48,8,512]{3,2,1,0:T(8,128)} %multiply_bitcast_fusion) | data formatting | bytes 25165824 | tf_op jit(solution)/shard_map/mul | solution.py:147
  469.7 168.8 %all-to-all-done = bf16[16,512,1024]{2,1,0:T(8,128)(2,1)} async-done(((bf16[16,512,1024]{2,1,0:T(8,128)(2,1)}), bf16[16,512,1024]{2,1,0:T(8,128)(2,1)}, u32[]{:S(2)}, u32[]{:S(2)}) %all-to-all-start) | async-done | bytes 16777248 | tf_op jit(solution)/shard_map/all_to_all | solution.py:78
  638.4 14.6 %add_convert_fusion = bf16[384,8192]{1,0:T(8,128)(2,1)} fusion(f32[384,8192]{1,0:T(8,128)} %bitcast.57, bf16[384,1024]{1,0:T(8,128)(2,1)S(1)} %copy-done.6, bf16[8192,1024]{1,0:T(8,128)(2,1)} %bitcast), kind=kOutput, calls=%fused_computation.2 | convolution fusion | flops 6448742400 | bytes 36438016 | tf_op jit(solution)/shard_map/dot_general | solution.py:82
  653.0 12.8 %add_convert_fusion.1 = bf16[384,1024]{1,0:T(8,128)(2,1)} fusion(f32[384,1024]{1,0:T(8,128)S(1)} %copy-done.4, bf16[384,8192]{1,0:T(8,128)(2,1)} %param.7, bf16[8192,1024]{1,0:T(8,128)(2,1)} %bitcast), kind=kOutput, calls=%fused_computation.12 | convolution fusion | flops 6443237376 | bytes 25427968 | tf_op jit(solution)/shard_map/dot_general | solution.py:81
  (63 shorter events, 47.2 us)
Async XLA Ops:
  9.5 20.7 %all-to-all-start.4 = ((bf16[384,16,64]{0,2,1:T(8,128)(2,1)}), bf16[384,16,64]{0,2,1:T(8,128)(2,1)S(1)}, u32[]{:S(2)}, u32[]{:S(2)}) async-start(bf16[384,16,64]{0,2,1:T(8,128)(2,1)} %bitcast.11), calls=%async_computation.4 | async-start | bytes 1572864 | tf_op jit(solution)/shard_map/all_to_all | solution.py:96
  30.2 5.4 copy-start.8
  30.2 5.6 copy-start.7
  30.2 6.4 copy-start.9
  30.2 6.4 copy-start.10
  30.2 117.5 %all-to-all-start.1 = ((bf16[384,16,512]{2,0,1:T(8,128)(2,1)}), bf16[384,16,512]{2,0,1:T(8,128)(2,1)}, u32[]{:S(2)}, u32[]{:S(2)}) async-start(bf16[384,16,512]{2,0,1:T(8,128)(2,1)} %bitcast.55), calls=%async_computation.1 | async-start | bytes 12582912 | tf_op jit(solution)/shard_map/all_to_all | solution.py:95
  35.6 102.5 %all-gather.3.cloned.1.call-start = ((), (), s32[]{:S(2)}) async-start(), calls=%async_computation.8 | async-start | bytes 2949120 | tf_op jit(solution)/shard_map/all_gather | solution.py:15
  36.5 244.6 %all-reduce.3.cloned.1.call-start = ((), (), s32[]{:S(2)}) async-start(), calls=%async_computation.10 | async-start | bytes 6291456 | tf_op jit(solution)/shard_map/psum | solution.py:107
  138.1 2.8 copy-start.2
  289.9 16.2 %all-to-all-start.2 = ((bf16[16,192,64]{1,2,0:T(8,128)(2,1)}), bf16[16,192,64]{1,2,0:T(8,128)(2,1)}, u32[]{:S(2)}, u32[]{:S(2)}) async-start(bf16[16,192,64]{1,2,0:T(8,128)(2,1)} %copy.39), calls=%async_computation.2 | async-start | bytes 1048576 | tf_op jit(solution)/shard_map/all_to_all | solution.py:53
  306.1 14.4 %all-to-all-start.3 = ((bf16[16,192,64]{1,2,0:T(8,128)(2,1)}), bf16[16,192,64]{1,2,0:T(8,128)(2,1)S(1)}, u32[]{:S(2)}, u32[]{:S(2)}) async-start(bf16[16,192,64]{1,2,0:T(8,128)(2,1)} %copy.40), calls=%async_computation.3 | async-start | bytes 1048576 | tf_op jit(solution)/shard_map/all_to_all | solution.py:53
  320.5 0.8 copy-start.3
  321.3 42.9 %copy-start = (bf16[16,192,512]{2,1,0:T(8,128)(2,1)S(1)}, bf16[16,192,512]{2,1,0:T(8,128)(2,1)}, u32[]{:S(2)}) copy-start(bf16[16,192,512]{2,1,0:T(8,128)(2,1)} %get-tuple-element.19) | copy-start | bytes 9437188
  364.2 42.4 %copy-start.5 = (bf16[512,1024]{1,0:T(8,128)(2,1)S(1)}, bf16[512,1024]{1,0:T(8,128)(2,1)}, u32[]{:S(2)}) copy-start(bf16[512,1024]{1,0:T(8,128)(2,1)} %param.8) | copy-start | bytes 3145732
  412.6 225.8 %all-to-all-start = ((bf16[16,512,1024]{2,1,0:T(8,128)(2,1)}), bf16[16,512,1024]{2,1,0:T(8,128)(2,1)}, u32[]{:S(2)}, u32[]{:S(2)}) async-start(bf16[16,512,1024]{2,1,0:T(8,128)(2,1)} %stack.2), calls=%async_computation | async-start | bytes 33554432 | tf_op jit(solution)/shard_map/all_to_all | solution.py:78
  418.7 247.1 %reduce-scatter.2.cloned.1.call-start = ((), (), s32[]{:S(2)}) async-start(), calls=%async_computation.9 | async-start | bytes 5898240 | tf_op jit(solution)/shard_map/reduce_scatter | solution.py:60
  425.4 2.2 copy-start.1
  458.2 180.2 %copy-start.6 = (bf16[384,1024]{1,0:T(8,128)(2,1)S(1)}, bf16[384,1024]{1,0:T(8,128)(2,1)}, u32[]{:S(2)}) copy-start(bf16[384,1024]{1,0:T(8,128)(2,1)} %param.11) | copy-start | bytes 2359300
  638.4 14.6 %copy-start.4 = (f32[384,1024]{1,0:T(8,128)S(1)}, f32[384,1024]{1,0:T(8,128)}, u32[]{:S(2)}) copy-start(f32[384,1024]{1,0:T(8,128)} %copy.41) | copy-start | bytes 4718596
Sparse Core Ops, SparseCore 0:
  39.3 76.9 all-gather.2
  154.1 126.9 all-reduce.2
  444.4 131.9 reduce-scatter.1
